TPU v7x, 32 devices: a whole 2x2x4 slice. The times are simulated.
32 devices in a mesh: fsdp: 2 (over y), tensor: 4 (over x, core), replica: 4 (over z).
Axes of the slice: x: 2, y: 2, z: 4, core: 2. Of those that a mesh axis runs over, the one named last changes fastest.
Arguments:
- gradient: bfloat16 [4, 4096, 8192], P('replica', 'fsdp', 'tensor'), may hold values from -400 to 400, as said below
- momentum: float32 [4, 4096, 8192], P('replica', 'fsdp', 'tensor'), may hold values from -6 to 6
- basis: float32 [8192, 256], P('tensor', 'fsdp'), may hold values from -0.0625 to 0.0625
Outputs:
- update: bfloat16 [4096, 8192], P('fsdp', 'tensor')
- momentum_new: float32 [4, 4096, 8192], P('replica', 'fsdp', 'tensor')
- basis_new: float32 [8192, 256], P('tensor', 'fsdp')
Inputs may be any that keep to these rules, and one draw needn't show every extreme that they name: gradient entries are finite real numbers.
All inputs are finite; a program needn't handle non-finite values.
Results may differ from a plain program's by a relative error of at most 0.001.
Values sent between devices are 32-bit elements; how exact they have to be, the bound alone decides.
A program may use at most 128 MiB of HBM per device.

v0:
```python
import jax
import jax.numpy as jnp
from jax import lax
from jax.sharding import PartitionSpec as P

M_ROWS = 4096
NCOLS = 8192
RANK = 256
HIGH = lax.Precision.HIGHEST


def local(gradient, momentum, basis):
    replicas = lax.axis_size("replica")
    rank_local = basis.shape[1]
    buffer = momentum[0] + gradient[0].astype(jnp.float32)
    partial_value = jnp.dot(
        buffer,
        lax.all_gather(basis, "fsdp", axis=1, tiled=True),
        precision=HIGH,
        preferred_element_type=jnp.float32,
    )
    left = lax.psum(partial_value, ("tensor", "replica")) / replicas
    local_gram = jnp.dot(left.T, left, precision=HIGH, preferred_element_type=jnp.float32)
    gram = lax.psum(local_gram, "fsdp")
    chol = jnp.linalg.cholesky(gram)
    ortho = lax.linalg.triangular_solve(chol, left, left_side=False, lower=True, transpose_a=True)
    right_part = jnp.dot(buffer.T, ortho, precision=HIGH, preferred_element_type=jnp.float32)
    right = lax.psum(right_part, ("fsdp", "replica")) / replicas
    squares = lax.psum(jnp.sum(right * right, axis=0), "tensor")
    norms = jnp.sqrt(squares + 1e-12)
    basis_full = right / norms
    lowrank = jnp.dot(ortho, right.T, precision=HIGH, preferred_element_type=jnp.float32)
    momentum_new = (buffer - 0.05 * lowrank)[None]
    scale = (M_ROWS * NCOLS / RANK) ** 0.5
    update = (
        scale * jnp.dot(ortho, basis_full.T, precision=HIGH, preferred_element_type=jnp.float32)
    ).astype(jnp.bfloat16)
    offset = lax.axis_index("fsdp") * rank_local
    basis_new = lax.dynamic_slice_in_dim(basis_full, offset, rank_local, 1)
    return (update, momentum_new, basis_new)


def solution(mesh):
    return jax.shard_map(
        local,
        mesh=mesh,
        in_specs=(
            P("replica", "fsdp", "tensor"),
            P("replica", "fsdp", "tensor"),
            P("tensor", "fsdp"),
        ),
        out_specs=(P("fsdp", "tensor"), P("replica", "fsdp", "tensor"), P("tensor", "fsdp")),
        check_vma=False,
    )
```

profile of v0, /device:TPU:0, one launch (start us, length us, event | category | flops | bytes accessed | tf_op | source)
XLA Modules:
  0.0 472.0 jit_solution(12130268575645546304)
XLA Ops:
  7.2 0.0 all-gather.2.cloned.1.call-start
  7.2 0.7 all-gather.2.cloned.1.call-update
  7.9 0.0 all-reduce.5.cloned.1.call-start
  7.9 37.4 %all-gather.2.cloned.1.call-done = f32[2048,256]{1,0:T(8,128)} async-done(((f32[2048,128]{1,0:T(8,128)}), f32[2048,256]{1,0:T(8,128)}) %all-gather.2.cloned.1.call-update) | async-done | bytes 2097168 | tf_op jit(solution)/shard_map/all_gather | solution.py:18
  45.3 18.8 %fusion.2 = f32[2048,256]{1,0:T(8,128)} fusion(f32[2048,256]{1,0:T(8,128)} %all-gather.2.cloned.1.call-done, f32[1,2048,2048]{2,1,0:T(8,128)} %param.4, bf16[1,2048,2048]{2,1,0:T(8,128)(2,1)} %param.3), kind=kOutput, calls=%fused_computation.5 | convolution fusion | flops 12893290496 | bytes 29360128 | tf_op jit(solution)/shard_map/dot_general | solution.py:16
  64.2 0.0 all-reduce.5.cloned.1.call-update
  64.2 0.0 all-reduce.7.cloned.1.call-start
  64.3 98.4 %all-reduce.5.cloned.1.call-done = f32[2048,256]{1,0:T(8,128)} async-done(((f32[2048,256]{1,0:T(8,128)}), f32[2048,256]{1,0:T(8,128)}) %all-reduce.5.cloned.1.call-update) | async-done | bytes 2097168 | tf_op jit(solution)/shard_map/psum | solution.py:22
  162.6 6.4 %fusion.19 = f32[256,256]{0,1:T(8,128)} fusion(f32[2048,256]{1,0:T(8,128)} %all-reduce.5.cloned.1.call-done), kind=kOutput, calls=%fused_computation.47 | convolution fusion | flops 1611137024 | bytes 2359296 | tf_op jit(solution)/shard_map/dot_general | solution.py:23
  169.0 0.0 all-reduce.7.cloned.1.call-update
  169.1 0.6 all-reduce.9.cloned.1.call-start
  169.6 1.7 broadcast_multiply_fusion
  171.4 20.4 %all-reduce.7.cloned.1.call-done = f32[256,256]{0,1:T(8,128)} async-done(((f32[256,256]{0,1:T(8,128)}), f32[256,256]{0,1:T(8,128)}) %all-reduce.7.cloned.1.call-update) | async-done | bytes 262160 | tf_op jit(solution)/shard_map/psum | solution.py:24
  191.7 1.1 copy.7
  192.8 1.0 fusion.9
  193.8 11.7 %cholesky.50 = f32[128,128]{1,0:T(8,128)S(1)} custom-call(f32[128,128]{1,0:T(8,128)S(1)} %cholesky.118), custom_call_target="Cholesky" | custom-call | tf_op jit(solution)/shard_map/jit(cholesky)/cholesky | solution.py:25
  205.6 9.8 %custom-call.14 = f32[1,128,128]{1,2,0:T(8,128)S(1)} custom-call(f32[1,128,128]{2,1,0:T(8,128)S(1)} %get-tuple-element.24), custom_call_target="InvertDiagBlocksLowerTriangular" | custom-call | tf_op jit(solution)/shard_map/jit(cholesky)/cholesky | solution.py:25
  215.4 0.2 constant_dynamic-update-slice_fusion
  215.6 0.3 convolution_subtract_fusion.1
  215.9 11.7 %cholesky.105 = f32[128,128]{1,0:T(8,128)S(1)} custom-call(f32[128,128]{1,0:T(8,128)S(1)} %convolution_subtract_fusion.1), custom_call_target="Cholesky" | custom-call | tf_op jit(solution)/shard_map/jit(cholesky)/cholesky | solution.py:25
  227.6 0.6 compare_reduce_fusion
  229.6 0.1 triangular_solve.58
  229.7 4.2 while.1
  229.9 0.6 fusion.28
  230.5 1.4 bitcast_dynamic-update-slice_fusion.2
  231.9 0.6 fusion.28
  232.5 1.4 bitcast_dynamic-update-slice_fusion.2
  233.9 19.7 %custom-call.15 = f32[2,128,128]{1,2,0:T(8,128)S(1)} custom-call(f32[2,128,128]{2,1,0:T(8,128)S(1)} %get-tuple-element.10), custom_call_target="InvertDiagBlocksLowerTriangular" | custom-call | tf_op jit(solution)/shard_map/triangular_solve | solution.py:26
  253.5 1.1 fusion.6
  254.6 1.8 convolution_subtract_fusion
  256.5 1.1 fusion.10
  257.6 0.0 copy-start.1
  257.6 1.0 copy-done.1
  258.5 31.3 %fusion = f32[2048,256]{1,0:T(8,128)} fusion(f32[1,2048,2048]{2,1,0:T(8,128)} %param.4, bf16[1,2048,2048]{2,1,0:T(8,128)(2,1)} %param.3, f32[2048,128]{0,1:T(8,128)S(1)} %fusion.10, f32[2048,128]{0,1:T(8,128)S(1)} %fusion.6), kind=kOutput, calls=%fused_computation.3 | convolution fusion | flops 12893814784 | bytes 29360128 | tf_op jit(solution)/shard_map/dot_general | solution.py:27
  289.8 0.0 all-reduce.9.cloned.1.call-update
  289.8 102.4 %all-reduce.9.cloned.1.call-done = f32[2048,256]{1,0:T(8,128)} async-done(((f32[2048,256]{1,0:T(8,128)}), f32[2048,256]{1,0:T(8,128)}) %all-reduce.9.cloned.1.call-update) | async-done | bytes 2097168 | tf_op jit(solution)/shard_map/psum | solution.py:28
  392.3 0.0 copy-start
  392.3 2.0 multiply_reduce_fusion
  394.3 6.4 %psum.31 = f32[256]{0:T(256)S(1)} all-reduce(f32[256]{0:T(256)S(1)} %multiply_reduce_fusion), channel_id=1, replica_groups=mesh['fsdp'=2,'tensor'=4,'replica'=4] {'tensor'}, use_global_device_ids=true, to_apply=%region_8.9 | all-reduce | flops 256 | bytes 2048 | tf_op jit(solution)/shard_map/psum | solution.py:29
  400.7 0.0 copy-done
  400.7 0.0 copy-start.2
  400.7 0.1 multiply_divide_fusion
  400.9 1.1 copy-done.2
  401.9 28.8 %multiply_convert_fusion = bf16[2048,2048]{1,0:T(8,128)(2,1)} fusion(f32[2048,256]{1,0:T(8,128)S(1)} %multiply_divide_fusion, f32[2048,128]{0,1:T(8,128)S(1)} %copy-done.2, f32[2048,128]{0,1:T(8,128)S(1)} %fusion.6), kind=kOutput, calls=%fused_computation.8 | convolution fusion | flops 12893814784 | bytes 12582912 | tf_op jit(solution)/shard_map/dot_general | solution.py:36
  430.8 1.0 constant_dynamic-slice_fusion.1
  431.8 33.1 %fusion.4 = f32[1,2048,2048]{2,1,0:T(8,128)} fusion(f32[1,2048,2048]{2,1,0:T(8,128)} %param.4, bf16[1,2048,2048]{2,1,0:T(8,128)(2,1)} %param.3, f32[2048,256]{1,0:T(8,128)S(1)} %copy-done, f32[2048,128]{0,1:T(8,128)S(1)} %copy-done.2, f32[2048,128]{0,1:T(8,128)S(1)} %fusion.6), kind=kOutput, calls=%fused_computation.7 | convolution fusion | flops 12902727680 | bytes 46137344 | tf_op jit(solution)/shard_map/dot_general | solution.py:32
  (10 shorter events, 0.2 us)
Async XLA Ops:
  7.2 38.2 %all-gather.2.cloned.1.call-start = ((), (), s32[]{:S(2)}) async-start(), calls=%async_computation | async-start | bytes 3145728 | tf_op jit(solution)/shard_map/all_gather | solution.py:18
  7.9 154.7 %all-reduce.5.cloned.1.call-start = ((), (), s32[]{:S(2)}) async-start(), calls=%async_computation.1 | async-start | bytes 4194304 | tf_op jit(solution)/shard_map/psum | solution.py:22
  64.2 127.5 %all-reduce.7.cloned.1.call-start = ((), (), s32[]{:S(2)}) async-start(), calls=%async_computation.2 | async-start | bytes 524288 | tf_op jit(solution)/shard_map/psum | solution.py:24
  169.1 223.2 %all-reduce.9.cloned.1.call-start = ((), (), s32[]{:S(2)}) async-start(), calls=%async_computation.3 | async-start | bytes 4194304 | tf_op jit(solution)/shard_map/psum | solution.py:28
  257.6 1.0 copy-start.1
  392.3 8.4 %copy-start = (f32[2048,256]{1,0:T(8,128)S(1)}, f32[2048,256]{1,0:T(8,128)}, u32[]{:S(2)}) copy-start(f32[2048,256]{1,0:T(8,128)} %all-reduce.9.cloned.1.call-done) | copy-start | bytes 6291460
  400.7 1.2 copy-start.2
Sparse Core Ops, SparseCore 0:
  9.5 35.7 all-gather.1
  64.3 98.2 all-reduce.4
  169.2 22.4 all-reduce.6
  289.9 102.2 all-reduce.8
where the time goes:
time: 478 us; the launch traced here: 472 us
  waiting for transfers between devices  259 us (54%)
  matrix products  123 us (26%)
  other arithmetic  58.6 us (12%)
  between operations  15.7 us (3%)
  local copies, waits for them, and re-layouts  8.2 us (2%)
  blocking collectives  6.38 us (1%)
    psum x1, waiting for transfers between devices, local(): right = lax.psum(right_part, ('fsdp', 'replica')) / replicas  102 us
    psum x1, waiting for transfers between devices, local(): left = lax.psum(partial_value, ('tensor', 'replica')) / replicas  98.4 us
    all_gather x1, waiting for transfers between devices, local(): lax.all_gather(basis, 'fsdp', axis=1, tiled=True)  37.4 us
    another operation x6, other arithmetic, local(): chol = jnp.linalg.cholesky(gram)  34 us
    dot_general x1, matrix products, local(): jnp.dot(ortho, right.T, precision=HIGH, preferred_element_type=jnp.float32)  33.1 us
    dot_general x1, matrix products, local(): jnp.dot(buffer.T, ortho, precision=HIGH, preferred_element_type=jnp.float32)  31.3 us
    dot_general x1, matrix products, local(): jnp.dot(ortho, basis_full.T, precision=HIGH, preferred_element_type=jnp.f...  28.8 us
    psum x1, waiting for transfers between devices, local(): gram = lax.psum(local_gram, 'fsdp')  20.4 us
  transfers between devices with their start and end apart: 4, of which 4 were waited for; matrix products, arithmetic and copies ran while one was open for 0% of the time, Pallas kernels for 0%

commit v1 on v0

--- a/solution.py
+++ b/solution.py
@@ -2,6 +2,7 @@
 import jax.numpy as jnp
 from jax import lax
 from jax.sharding import PartitionSpec as P
+from jax.lax import psum
 
 M_ROWS = 4096
 NCOLS = 8192
@@ -19,7 +20,7 @@
         precision=HIGH,
         preferred_element_type=jnp.float32,
     )
-    left = lax.psum(partial_value, ("tensor", "replica")) / replicas
+    left = psum(psum(partial_value, "replica"), "tensor") / replicas
     local_gram = jnp.dot(left.T, left, precision=HIGH, preferred_element_type=jnp.float32)
     gram = lax.psum(local_gram, "fsdp")
     chol = jnp.linalg.cholesky(gram)

time: 478 us -> 520 us (1.088)
  waiting for transfers between devices: 259 us -> 301 us
    psum x1 -> x2, waiting for transfers between devices: 98.4 us -> 139 us  [local(): left = psum(psum(partial_value, 'replica'), 'tensor') / replicas]
  transfers between devices with their start and end apart: 4 -> 5, of which waited for: 4 -> 5; matrix products, arithmetic and copies ran while one was open for 0% -> 0% of each run, Pallas kernels for 0% -> 0%
where the time goes in v1:
time: 520 us; the launch traced here: 514 us
  waiting for transfers between devices  301 us (58%)
  matrix products  123 us (24%)
  other arithmetic  58.6 us (11%)
  between operations  15.7 us (3%)
  local copies, waits for them, and re-layouts  8.2 us (2%)
  blocking collectives  6.38 us (1%)
    psum x2, waiting for transfers between devices, local(): left = psum(psum(partial_value, 'replica'), 'tensor') / replicas  139 us
    psum x1, waiting for transfers between devices, local(): right = lax.psum(right_part, ('fsdp', 'replica')) / replicas  102 us
    all_gather x1, waiting for transfers between devices, local(): lax.all_gather(basis, 'fsdp', axis=1, tiled=True)  37.4 us
    another operation x6, other arithmetic, local(): chol = jnp.linalg.cholesky(gram)  34 us
    dot_general x1, matrix products, local(): jnp.dot(ortho, right.T, precision=HIGH, preferred_element_type=jnp.float32)  33.1 us
    dot_general x1, matrix products, local(): jnp.dot(buffer.T, ortho, precision=HIGH, preferred_element_type=jnp.float32)  31.3 us
    dot_general x1, matrix products, local(): jnp.dot(ortho, basis_full.T, precision=HIGH, preferred_element_type=jnp.f...  28.8 us
    psum x1, waiting for transfers between devices, local(): gram = lax.psum(local_gram, 'fsdp')  21.2 us
  transfers between devices with their start and end apart: 5, of which 5 were waited for; matrix products, arithmetic and copies ran while one was open for 0% of the time, Pallas kernels for 0%

profile of v1, /device:TPU:0, one launch (start us, length us, event | category | flops | bytes accessed | tf_op | source)
XLA Modules:
  0.0 513.5 jit_solution(10190933296312721603)
XLA Ops:
  7.2 0.0 all-gather.2.cloned.1.call-start
  7.2 0.7 all-gather.2.cloned.1.call-update
  7.9 0.0 all-reduce.6.cloned.1.call-start
  7.9 37.4 %all-gather.2.cloned.1.call-done = f32[2048,256]{1,0:T(8,128)} async-done(((f32[2048,128]{1,0:T(8,128)}), f32[2048,256]{1,0:T(8,128)}) %all-gather.2.cloned.1.call-update) | async-done | bytes 2097168 | tf_op jit(solution)/shard_map/all_gather | solution.py:19
  45.3 18.8 %fusion.2 = f32[2048,256]{1,0:T(8,128)} fusion(f32[2048,256]{1,0:T(8,128)} %all-gather.2.cloned.1.call-done, f32[1,2048,2048]{2,1,0:T(8,128)} %param.4, bf16[1,2048,2048]{2,1,0:T(8,128)(2,1)} %param.3), kind=kOutput, calls=%fused_computation.5 | convolution fusion | flops 12893290496 | bytes 29360128 | tf_op jit(solution)/shard_map/dot_general | solution.py:17
  64.2 0.0 all-reduce.6.cloned.1.call-update
  64.2 0.0 all-reduce.8.cloned.1.call-start
  64.2 86.3 %all-reduce.6.cloned.1.call-done = f32[2048,256]{1,0:T(8,128)} async-done(((f32[2048,256]{1,0:T(8,128)}), f32[2048,256]{1,0:T(8,128)}) %all-reduce.6.cloned.1.call-update) | async-done | bytes 2097168 | tf_op jit(solution)/shard_map/psum | solution.py:23
  150.5 0.0 all-reduce.8.cloned.1.call-update
  150.5 0.0 all-reduce.10.cloned.1.call-start
  150.6 52.7 %all-reduce.8.cloned.1.call-done = f32[2048,256]{1,0:T(8,128)} async-done(((f32[2048,256]{1,0:T(8,128)}), f32[2048,256]{1,0:T(8,128)}) %all-reduce.8.cloned.1.call-update) | async-done | bytes 2097168 | tf_op jit(solution)/shard_map/psum | solution.py:23
  203.3 6.4 %fusion.19 = f32[256,256]{0,1:T(8,128)} fusion(f32[2048,256]{1,0:T(8,128)} %all-reduce.8.cloned.1.call-done), kind=kOutput, calls=%fused_computation.47 | convolution fusion | flops 1611137024 | bytes 2359296 | tf_op jit(solution)/shard_map/dot_general | solution.py:24
  209.7 0.0 all-reduce.10.cloned.1.call-update
  209.7 0.6 all-reduce.12.cloned.1.call-start
  210.3 1.7 broadcast_multiply_fusion
  212.0 21.2 %all-reduce.10.cloned.1.call-done = f32[256,256]{0,1:T(8,128)} async-done(((f32[256,256]{0,1:T(8,128)}), f32[256,256]{0,1:T(8,128)}) %all-reduce.10.cloned.1.call-update) | async-done | bytes 262160 | tf_op jit(solution)/shard_map/psum | solution.py:25
  233.3 1.1 copy.7
  234.4 1.0 fusion.9
  235.4 11.7 %cholesky.50 = f32[128,128]{1,0:T(8,128)S(1)} custom-call(f32[128,128]{1,0:T(8,128)S(1)} %cholesky.118), custom_call_target="Cholesky" | custom-call | tf_op jit(solution)/shard_map/jit(cholesky)/cholesky | solution.py:26
  247.1 9.8 %custom-call.14 = f32[1,128,128]{1,2,0:T(8,128)S(1)} custom-call(f32[1,128,128]{2,1,0:T(8,128)S(1)} %get-tuple-element.24), custom_call_target="InvertDiagBlocksLowerTriangular" | custom-call | tf_op jit(solution)/shard_map/jit(cholesky)/cholesky | solution.py:26
  256.9 0.2 constant_dynamic-update-slice_fusion
  257.2 0.3 convolution_subtract_fusion.1
  257.4 11.7 %cholesky.105 = f32[128,128]{1,0:T(8,128)S(1)} custom-call(f32[128,128]{1,0:T(8,128)S(1)} %convolution_subtract_fusion.1), custom_call_target="Cholesky" | custom-call | tf_op jit(solution)/shard_map/jit(cholesky)/cholesky | solution.py:26
  269.2 0.6 compare_reduce_fusion
  271.2 0.1 triangular_solve.58
  271.2 4.2 while.1
  271.4 0.6 fusion.28
  272.0 1.4 bitcast_dynamic-update-slice_fusion.2
  273.4 0.6 fusion.28
  274.0 1.4 bitcast_dynamic-update-slice_fusion.2
  275.4 19.7 %custom-call.15 = f32[2,128,128]{1,2,0:T(8,128)S(1)} custom-call(f32[2,128,128]{2,1,0:T(8,128)S(1)} %get-tuple-element.10), custom_call_target="InvertDiagBlocksLowerTriangular" | custom-call | tf_op jit(solution)/shard_map/triangular_solve | solution.py:27
  295.1 1.1 fusion.6
  296.2 1.8 convolution_subtract_fusion
  298.0 1.1 fusion.10
  299.1 0.0 copy-start.1
  299.1 1.0 copy-done.1
  300.1 31.3 %fusion = f32[2048,256]{1,0:T(8,128)} fusion(f32[1,2048,2048]{2,1,0:T(8,128)} %param.4, bf16[1,2048,2048]{2,1,0:T(8,128)(2,1)} %param.3, f32[2048,128]{0,1:T(8,128)S(1)} %fusion.10, f32[2048,128]{0,1:T(8,128)S(1)} %fusion.6), kind=kOutput, calls=%fused_computation.3 | convolution fusion | flops 12893814784 | bytes 29360128 | tf_op jit(solution)/shard_map/dot_general | solution.py:28
  331.3 0.0 all-reduce.12.cloned.1.call-update
  331.4 102.4 %all-reduce.12.cloned.1.call-done = f32[2048,256]{1,0:T(8,128)} async-done(((f32[2048,256]{1,0:T(8,128)}), f32[2048,256]{1,0:T(8,128)}) %all-reduce.12.cloned.1.call-update) | async-done | bytes 2097168 | tf_op jit(solution)/shard_map/psum | solution.py:29
  433.8 0.0 copy-start
  433.8 2.0 multiply_reduce_fusion
  435.8 6.4 %psum.39 = f32[256]{0:T(256)S(1)} all-reduce(f32[256]{0:T(256)S(1)} %multiply_reduce_fusion), channel_id=1, replica_groups=mesh['fsdp'=2,'tensor'=4,'replica'=4] {'tensor'}, use_global_device_ids=true, to_apply=%region_9.10 | all-reduce | flops 256 | bytes 2048 | tf_op jit(solution)/shard_map/psum | solution.py:30
  442.2 0.0 copy-done
  442.2 0.0 copy-start.2
  442.2 0.1 multiply_divide_fusion
  442.4 1.1 copy-done.2
  443.5 28.8 %multiply_convert_fusion = bf16[2048,2048]{1,0:T(8,128)(2,1)} fusion(f32[2048,256]{1,0:T(8,128)S(1)} %multiply_divide_fusion, f32[2048,128]{0,1:T(8,128)S(1)} %copy-done.2, f32[2048,128]{0,1:T(8,128)S(1)} %fusion.6), kind=kOutput, calls=%fused_computation.8 | convolution fusion | flops 12893814784 | bytes 12582912 | tf_op jit(solution)/shard_map/dot_general | solution.py:37
  472.3 1.0 constant_dynamic-slice_fusion.1
  473.3 33.1 %fusion.4 = f32[1,2048,2048]{2,1,0:T(8,128)} fusion(f32[1,2048,2048]{2,1,0:T(8,128)} %param.4, bf16[1,2048,2048]{2,1,0:T(8,128)(2,1)} %param.3, f32[2048,256]{1,0:T(8,128)S(1)} %copy-done, f32[2048,128]{0,1:T(8,128)S(1)} %copy-done.2, f32[2048,128]{0,1:T(8,128)S(1)} %fusion.6), kind=kOutput, calls=%fused_computation.7 | convolution fusion | flops 12902727680 | bytes 46137344 | tf_op jit(solution)/shard_map/dot_general | solution.py:33
  (10 shorter events, 0.2 us)
Async XLA Ops:
  7.2 38.2 %all-gather.2.cloned.1.call-start = ((), (), s32[]{:S(2)}) async-start(), calls=%async_computation | async-start | bytes 3145728 | tf_op jit(solution)/shard_map/all_gather | solution.py:19
  7.9 142.6 %all-reduce.6.cloned.1.call-start = ((), (), s32[]{:S(2)}) async-start(), calls=%async_computation.1 | async-start | bytes 4194304 | tf_op jit(solution)/shard_map/psum | solution.py:23
  64.2 139.1 %all-reduce.8.cloned.1.call-start = ((), (), s32[]{:S(2)}) async-start(), calls=%async_computation.2 | async-start | bytes 4194304 | tf_op jit(solution)/shard_map/psum | solution.py:23
  150.5 82.7 %all-reduce.10.cloned.1.call-start = ((), (), s32[]{:S(2)}) async-start(), calls=%async_computation.3 | async-start | bytes 524288 | tf_op jit(solution)/shard_map/psum | solution.py:25
  209.7 224.1 %all-reduce.12.cloned.1.call-start = ((), (), s32[]{:S(2)}) async-start(), calls=%async_computation.4 | async-start | bytes 4194304 | tf_op jit(solution)/shard_map/psum | solution.py:29
  299.1 1.0 copy-start.1
  433.8 8.4 %copy-start = (f32[2048,256]{1,0:T(8,128)S(1)}, f32[2048,256]{1,0:T(8,128)}, u32[]{:S(2)}) copy-start(f32[2048,256]{1,0:T(8,128)} %all-reduce.12.cloned.1.call-done) | copy-start | bytes 6291460
  442.2 1.2 copy-start.2
Sparse Core Ops, SparseCore 0:
  9.5 35.7 all-gather.1
  64.3 86.1 all-reduce.5
  152.9 50.3 all-reduce.7
  209.9 23.3 all-reduce.9
  331.5 102.2 all-reduce.11
